TPU v7x, 256 devices: a whole 4x4x8 slice. The times are simulated.
256 devices in a mesh: slab: 4 (over x), panel: 64 (over z, y, core).
Axes of the slice: x: 4, y: 4, z: 8, core: 2. Of those that a mesh axis runs over, the one named last changes fastest.
Arguments:
- trial: bfloat16 [1600, 6400], P('slab', 'panel'), may hold values from -6 to 6
- integrals: bfloat16 [6400, 256, 300], P(None, 'panel'), may hold values from -0.078125 to 0.078125
- basis: bfloat16 [2, 1600, 256, 300], P(None, 'slab', 'panel'), may hold values from -0.00048828125 to 0.00048828125
- images: bfloat16 [2, 1600, 256, 300], P(None, 'slab', 'panel'), may hold values from -6 to 6
- current: bfloat16 [1600, 256, 300], P('slab', 'panel'), may hold values from -18 to 18
- occ_energy: float32 [40], replicated, may hold values from -1 to -0.3
- vir_energy: float32 [300], replicated, may hold values from 0.1 to 2
- shift: float32 [1], replicated, may hold values from 0.5 to 1.5
Outputs:
- sigma: bfloat16 [1600, 256, 300], P('slab', 'panel')
- update: bfloat16 [1600, 256, 300], P('slab', 'panel')
- correlations: float32 [2], replicated
All inputs are finite; a program needn't handle non-finite values.
Results may differ from a plain program's by a relative error of at most 0.0079.
Values may be sent and summed in bfloat16 or wider, within the bound.
No kernel may reach another device: no remote copies, remote signals or barrier semaphores. Data moves between devices by JAX's collectives and lax.ppermute only.
A program may use at most 128 MiB of HBM per device.

v0:
```python
import jax
import jax.numpy as jnp
from jax import lax
from jax.sharding import PartitionSpec as P

OCCUPIED = 40


def per_device(trial, integrals, basis, images, current, occ_energy, vir_energy, shift):
    rows = trial.shape[0]
    width_b = integrals.shape[1]
    virtuals = integrals.shape[2]
    flat = integrals.reshape(integrals.shape[0], width_b * virtuals)
    whole = lax.all_gather(trial, "panel", axis=1, tiled=True)
    summed = jnp.dot(whole, flat, preferred_element_type=jnp.float32)
    sigma = summed.astype(jnp.bfloat16).reshape(rows, width_b, virtuals)
    sig_full = sigma.astype(jnp.float32)
    count = basis.shape[0]
    local_over = jnp.einsum(
        "kn,n->k", basis.reshape(count, -1), sigma.reshape(-1), preferred_element_type=jnp.float32
    )
    global_row = lax.axis_index("slab") * rows + jnp.arange(rows, dtype=jnp.int32)
    first_occ = global_row // OCCUPIED
    second_occ = global_row % OCCUPIED
    orbitals = jnp.arange(OCCUPIED, dtype=jnp.int32)
    energy_first = jnp.sum(
        jnp.where(first_occ[:, None] == orbitals[None, :], occ_energy[None, :], 0.0), axis=1
    )
    energy_second = jnp.sum(
        jnp.where(second_occ[:, None] == orbitals[None, :], occ_energy[None, :], 0.0), axis=1
    )
    pair_energy = energy_first + energy_second
    energy_b = lax.dynamic_slice_in_dim(vir_energy, lax.axis_index("panel") * width_b, width_b, 0)
    denom = jnp.maximum(
        vir_energy[None, None, :] + energy_b[None, :, None] - pair_energy[:, None, None] - shift[0],
        1.0,
    )
    scaled_current = current.astype(jnp.float32)
    correlations = lax.psum(local_over, ("slab", "panel"))
    resid = sig_full - shift[0] * scaled_current
    for index in range(count):
        resid = resid - correlations[index] * images[index].astype(jnp.float32)
    delta = resid / denom
    size_sq = lax.psum(jnp.sum(delta * delta), ("slab", "panel"))
    update = (delta * lax.rsqrt(size_sq + 1e-06)).astype(jnp.bfloat16)
    return (sigma, update, correlations)


def solution(mesh):
    in_specs = (
        P("slab", "panel"),
        P(None, "panel", None),
        P(None, "slab", "panel", None),
        P(None, "slab", "panel", None),
        P("slab", "panel", None),
        P(),
        P(),
        P(),
    )
    out_specs = (P("slab", "panel", None), P("slab", "panel", None), P())
    return jax.shard_map(
        per_device, mesh=mesh, in_specs=in_specs, out_specs=out_specs, check_vma=False
    )
```

profile of v0, /device:TPU:1, one launch (start us, length us, event | category | flops | bytes accessed | tf_op | source)
XLA Modules:
  0.0 309.0 jit_solution(7445834770455601225)
XLA Ops:
  7.2 0.0 all-gather.3.cloned.1.call-start
  7.2 0.7 all-gather.3.cloned.1.call-update
  7.9 15.1 %copy.16 = bf16[6400,4,300]{0,2,1:T(8,128)(2,1)} copy(bf16[6400,4,300]{0,1,2:T(4,128)(2,1)} %param.9) | data formatting | bytes 30720000 | tf_op args[1]
  23.0 16.0 %reshape.77 = bf16[6400,1200]{0,1:T(8,128)(2,1)} reshape(bf16[6400,4,300]{0,2,1:T(8,128)(2,1)} %copy.16) | data formatting | bytes 30720000 | tf_op jit(solution)/shard_map/reshape | solution.py:13
  39.0 5.8 %reshape.85 = bf16[960000]{0:T(1024)(128)(2,1)S(1)} reshape(bf16[2,400,4,300]{3,2,1,0:T(4,128)(2,1)} %param.10) | data formatting | bytes 3840000
  44.8 0.0 copy-start.3
  44.8 0.0 copy-start.1
  44.8 4.0 %reshape.79 = bf16[2,480000]{1,0:T(2,128)(2,1)} reshape(bf16[960000]{0:T(1024)(128)(2,1)S(1)} %reshape.85) | data formatting | bytes 3840000 | tf_op jit(solution)/shard_map/reshape | solution.py:20
  49.5 0.0 copy-done.3
  49.5 0.1 select_reduce_fusion
  49.6 0.0 copy-done.1
  49.6 0.1 dynamic_slice.3
  49.7 0.1 broadcast_add_fusion
  49.8 45.9 %all-gather.3.cloned.1.call-done = bf16[64,100,400]{1,2,0:T(8,128)(2,1)} async-done(((bf16[1,100,400]{1,2,0:T(8,128)(2,1)}), bf16[64,100,400]{1,2,0:T(8,128)(2,1)}) %all-gather.3.cloned.1.call-update) | async-done | bytes 5120016 | tf_op jit(solution)/shard_map/all_gather | solution.py:14
  95.7 7.3 %copy.15 = bf16[64,100,400]{1,0,2:T(8,128)(2,1)} copy(bf16[64,100,400]{1,2,0:T(8,128)(2,1)} %all-gather.3.cloned.1.call-done) | data formatting | bytes 10240000 | tf_op jit(solution)/shard_map/all_gather | solution.py:14
  103.0 13.1 %reshape.81 = bf16[6400,400]{0,1:T(8,128)(2,1)} reshape(bf16[64,100,400]{1,0,2:T(8,128)(2,1)} %copy.15) | data formatting | bytes 10240000
  116.1 15.8 %convolution_convert_fusion = bf16[400,1200]{1,0:T(8,128)(2,1)S(1)} fusion(bf16[6400,400]{0,1:T(8,128)(2,1)} %reshape.81, bf16[6400,1200]{0,1:T(8,128)(2,1)} %reshape.77), kind=kOutput, calls=%fused_computation | convolution fusion | flops 6144480256 | bytes 21440000 | tf_op jit(solution)/shard_map/dot_general | solution.py:15
  131.9 0.0 copy-start
  131.9 4.6 %reshape.82 = bf16[480000,1]{0,1:T(2,128)(2,1)} reshape(bf16[400,1200]{1,0:T(8,128)(2,1)S(1)} %convolution_convert_fusion) | data formatting | bytes 1920000 | tf_op jit(solution)/shard_map/reshape;reshape | solution.py:20
  136.6 0.0 copy-done
  136.6 5.6 %convolution_bitcast_fusion = f32[2]{0:T(128)S(1)} fusion(bf16[480000,1]{0,1:T(2,128)(2,1)} %reshape.82, bf16[2,480000]{1,0:T(2,128)(2,1)S(1)} %copy-done), kind=kOutput, calls=%fused_computation.6 | convolution fusion | flops 1920000 | bytes 2880008 | tf_op jit(solution)/shard_map/kn,n->k/dot_general | solution.py:19
  142.2 2.0 reshape.78
  144.2 74.6 %psum.14 = f32[2]{0:T(128)S(1)} all-reduce(f32[2]{0:T(128)S(1)} %convolution_bitcast_fusion), channel_id=1, replica_groups=mesh['slab'=4,'panel'=64] {'slab','panel'}, use_global_device_ids=true, to_apply=%region_0.1 | all-reduce | flops 2 | bytes 16 | tf_op jit(solution)/shard_map/psum | solution.py:39
  218.7 0.0 copy-start.2
  218.7 0.7 fusion.7
  219.4 7.3 %multiply_reduce_fusion = (f32[]{:T(128)}, f32[400,4,300]{2,1,0:T(4,128)S(1)}) fusion(f32[400]{0:T(512)S(1)} %add.70, f32[4,300]{1,0:T(4,128)S(1)} %broadcast_add_fusion, bf16[2,400,4,300]{3,2,1,0:T(4,128)(2,1)} %param.11, f32[]{:T(128)} %bitcast.6, f32[]{:T(128)} %bitcast.4, bf16[400,4,300]{2,1,0:T(4,128)(2,1)} %param.12, f32[]{:T(128)} %bitcast.26, ...), kind=kLoop, calls=%fused_computation.5 | loop fusion | flops 7679999 | bytes 5766416 | tf_op jit(solution)/shard_map/reduce_sum | solution.py:44
  226.7 0.0 copy-done.2
  226.7 73.4 %psum.15 = f32[]{:T(128)} all-reduce(f32[]{:T(128)} %get-tuple-element.5), channel_id=1, replica_groups=mesh['slab'=4,'panel'=64] {'slab','panel'}, use_global_device_ids=true, to_apply=%region_4.5 | all-reduce | flops 1 | bytes 8 | tf_op jit(solution)/shard_map/psum | solution.py:44
  300.7 1.5 multiply_convert_fusion
  (2 shorter events, 0.0 us)
Async XLA Ops:
  7.2 88.5 %all-gather.3.cloned.1.call-start = ((), (), s32[]{:S(2)}) async-start(), calls=%async_computation | async-start | bytes 6656000 | tf_op jit(solution)/shard_map/all_gather | solution.py:14
  44.8 4.7 %copy-start.3 = (f32[40]{0:T(128)S(1)}, f32[40]{0:T(128)}, u32[]{:S(2)}) copy-start(f32[40]{0:T(128)} %param.13) | copy-start | bytes 484
  44.8 4.8 %copy-start.1 = (f32[300]{0:T(512)S(1)}, f32[300]{0:T(512)}, u32[]{:S(2)}) copy-start(f32[300]{0:T(512)} %param.14) | copy-start | bytes 3604
  131.9 4.6 %copy-start = (bf16[2,480000]{1,0:T(2,128)(2,1)S(1)}, bf16[2,480000]{1,0:T(2,128)(2,1)}, u32[]{:S(2)}) copy-start(bf16[2,480000]{1,0:T(2,128)(2,1)} %reshape.79) | copy-start | bytes 5760004
  218.7 7.9 %copy-start.2 = (f32[2]{0:T(128)}, f32[2]{0:T(128)S(1)}, u32[]{:S(2)}) copy-start(f32[2]{0:T(128)S(1)} %psum.14) | copy-start | bytes 28
Sparse Core Ops, SparseCore 0:
  10.7 85.0 all-gather.2
where the time goes:
time: 310 us; the launch traced here: 309 us
  blocking collectives  148 us (48%)
  local copies, waits for them, and re-layouts  68.7 us (22%)
  waiting for transfers between devices  46.6 us (15%)
  matrix products  21.4 us (7%)
  between operations  15.5 us (5%)
  other arithmetic  8.91 us (3%)
    psum x1, blocking collectives, per_device(): correlations = lax.psum(local_over, ('slab', 'panel'))  74.6 us
    psum x1, blocking collectives, per_device(): size_sq = lax.psum(jnp.sum(delta * delta), ('slab', 'panel'))  73.4 us
    all_gather x1, waiting for transfers between devices, per_device(): whole = lax.all_gather(trial, 'panel', axis=1, tiled=True)  45.9 us
    unnamed x11, local copies, waits for them, and re-layouts  34 us
    reshape x1, local copies, waits for them, and re-layouts, per_device(): flat = integrals.reshape(integrals.shape[0], width_b * virtuals)  16 us
    dot_general x1, matrix products, per_device(): summed = jnp.dot(whole, flat, preferred_element_type=jnp.float32)  15.8 us
    all_gather x1, local copies, waits for them, and re-layouts, per_device(): whole = lax.all_gather(trial, 'panel', axis=1, tiled=True)  7.3 us
    reduce_sum x1, other arithmetic, per_device(): size_sq = lax.psum(jnp.sum(delta * delta), ('slab', 'panel'))  7.26 us
  transfers between devices with their start and end apart: 1, of which 1 were waited for; matrix products, arithmetic and copies ran while one was open for 13% of the time, Pallas kernels for 0%

commit v1 on v0

--- a/solution.py
+++ b/solution.py
@@ -11,7 +11,9 @@
     width_b = integrals.shape[1]
     virtuals = integrals.shape[2]
     flat = integrals.reshape(integrals.shape[0], width_b * virtuals)
-    whole = lax.all_gather(trial, "panel", axis=1, tiled=True)
+    whole = jnp.concatenate(
+        lax.all_to_all(jnp.stack([trial] * lax.axis_size("panel")), "panel", 0, 0), axis=1
+    )
     summed = jnp.dot(whole, flat, preferred_element_type=jnp.float32)
     sigma = summed.astype(jnp.bfloat16).reshape(rows, width_b, virtuals)
     sig_full = sigma.astype(jnp.float32)

time: 310 us -> 373 us (1.20)
  waiting for transfers between devices: 46.6 us -> 103 us
  between operations: 15.5 us -> 2.07 us
  starting transfers between devices: 0.04 us -> 13.3 us
  local copies, waits for them, and re-layouts: 68.7 us -> 73.1 us
    all_to_all x0 -> x1, waiting for transfers between devices: none -> 103 us  [per_device(): lax.all_to_all(jnp.stack([trial] * lax.axis_size('panel')), 'panel', 0, 0)]
    all_gather x1 -> x0, waiting for transfers between devices: 45.9 us -> none  [per_device(): whole = lax.all_gather(trial, 'panel', axis=1, tiled=True)]
    reshape x0 -> x2, local copies, waits for them, and re-layouts: none -> 20.4 us  [per_device(): jnp.concatenate(lax.all_to_all(jnp.stack([trial] * lax.axis_size('panel')...]
    all_to_all x0 -> x1, starting transfers between devices: none -> 13.3 us  [per_device(): lax.all_to_all(jnp.stack([trial] * lax.axis_size('panel')), 'panel', 0, 0)]
    unnamed x11 -> x10, local copies, waits for them, and re-layouts: 34 us -> 20.9 us
    all_gather x1 -> x0, local copies, waits for them, and re-layouts: 7.3 us -> none  [per_device(): whole = lax.all_gather(trial, 'panel', axis=1, tiled=True)]
    another operation x0 -> x1, local copies, waits for them, and re-layouts: none -> 4.47 us  [per_device(): jnp.stack([trial] * lax.axis_size('panel'))]
  transfers between devices with their start and end apart: 1 -> 1, of which waited for: 1 -> 1; matrix products, arithmetic and copies ran while one was open for 13% -> 11% of each run, Pallas kernels for 0% -> 0%
where the time goes in v1:
time: 373 us; the launch traced here: 372 us
  blocking collectives  150 us (40%)
  waiting for transfers between devices  103 us (28%)
  local copies, waits for them, and re-layouts  73.1 us (20%)
  matrix products  21.4 us (6%)
  starting transfers between devices  13.3 us (4%)
  other arithmetic  8.91 us (2%)
    all_to_all x1, waiting for transfers between devices, per_device(): lax.all_to_all(jnp.stack([trial] * lax.axis_size('panel')), 'panel', 0, 0)  103 us
    psum x1, blocking collectives, per_device(): correlations = lax.psum(local_over, ('slab', 'panel'))  77.7 us
    psum x1, blocking collectives, per_device(): size_sq = lax.psum(jnp.sum(delta * delta), ('slab', 'panel'))  72.7 us
    unnamed x10, local copies, waits for them, and re-layouts  20.9 us
    reshape x2, local copies, waits for them, and re-layouts, per_device(): jnp.concatenate(lax.all_to_all(jnp.stack([trial] * lax.axis_size('panel')...  20.4 us
    reshape x1, local copies, waits for them, and re-layouts, per_device(): flat = integrals.reshape(integrals.shape[0], width_b * virtuals)  16 us
    dot_general x1, matrix products, per_device(): summed = jnp.dot(whole, flat, preferred_element_type=jnp.float32)  15.8 us
    all_to_all x1, starting transfers between devices, per_device(): lax.all_to_all(jnp.stack([trial] * lax.axis_size('panel')), 'panel', 0, 0)  13.3 us
  transfers between devices with their start and end apart: 1, of which 1 were waited for; matrix products, arithmetic and copies ran while one was open for 11% of the time, Pallas kernels for 0%

profile of v1, /device:TPU:1, one launch (start us, length us, event | category | flops | bytes accessed | tf_op | source)
XLA Modules:
  0.0 371.7 jit_solution(4186195578989407305)
XLA Ops:
  0.6 4.5 %stack.2 = bf16[64,400,100]{2,1,0:T(8,128)(2,1)} broadcast(bf16[400,100]{1,0:T(8,128)(2,1)} %param.8), dimensions={1,2} | broadcast | bytes 5200000 | tf_op jit(solution)/shard_map/stack | solution.py:15
  5.1 13.3 %all-to-all-start = ((bf16[64,400,100]{2,1,0:T(8,128)(2,1)}), bf16[64,400,100]{2,1,0:T(8,128)(2,1)}, u32[]{:S(2)}, u32[]{:S(2)}) async-start(bf16[64,400,100]{2,1,0:T(8,128)(2,1)} %stack.2), calls=%async_computation | async-start | bytes 13107200 | tf_op jit(solution)/shard_map/all_to_all | solution.py:15
  18.4 15.1 %copy.15 = bf16[6400,4,300]{0,2,1:T(8,128)(2,1)} copy(bf16[6400,4,300]{0,1,2:T(4,128)(2,1)} %param.9) | data formatting | bytes 30720000 | tf_op args[1]
  33.5 16.0 %reshape.87 = bf16[6400,1200]{0,1:T(8,128)(2,1)} reshape(bf16[6400,4,300]{0,2,1:T(8,128)(2,1)} %copy.15) | data formatting | bytes 30720000 | tf_op jit(solution)/shard_map/reshape | solution.py:13
  49.5 5.8 %reshape.93 = bf16[960000]{0:T(1024)(128)(2,1)S(1)} reshape(bf16[2,400,4,300]{3,2,1,0:T(4,128)(2,1)} %param.10) | data formatting | bytes 3840000
  55.3 0.0 copy-start.3
  55.3 0.0 copy-start.1
  55.3 4.0 %reshape.89 = bf16[2,480000]{1,0:T(2,128)(2,1)} reshape(bf16[960000]{0:T(1024)(128)(2,1)S(1)} %reshape.93) | data formatting | bytes 3840000 | tf_op jit(solution)/shard_map/reshape | solution.py:22
  60.0 0.0 copy-done.3
  60.0 0.1 select_reduce_fusion
  60.1 0.0 copy-done.1
  60.1 0.1 dynamic_slice.3
  60.2 0.1 broadcast_add_fusion
  60.3 102.5 %all-to-all-done = bf16[64,400,100]{2,1,0:T(8,128)(2,1)} async-done(((bf16[64,400,100]{2,1,0:T(8,128)(2,1)}), bf16[64,400,100]{2,1,0:T(8,128)(2,1)}, u32[]{:S(2)}, u32[]{:S(2)}) %all-to-all-start) | async-done | bytes 5120032 | tf_op jit(solution)/shard_map/all_to_all | solution.py:15
  162.8 7.3 %copy.14 = bf16[400,64,100]{2,1,0:T(8,128)(2,1)} copy(bf16[400,64,100]{2,0,1:T(8,128)(2,1)} %bitcast) | data formatting | bytes 10240000 | tf_op jit(solution)/shard_map/reshape | solution.py:14
  170.1 13.1 %reshape.86 = bf16[400,6400]{1,0:T(8,128)(2,1)} reshape(bf16[400,64,100]{2,1,0:T(8,128)(2,1)} %copy.14) | data formatting | bytes 10240000 | tf_op jit(solution)/shard_map/reshape | solution.py:14
  183.2 15.8 %convolution_convert_fusion = bf16[400,1200]{1,0:T(8,128)(2,1)S(1)} fusion(bf16[400,6400]{1,0:T(8,128)(2,1)} %reshape.86, bf16[6400,1200]{0,1:T(8,128)(2,1)} %reshape.87), kind=kOutput, calls=%fused_computation | convolution fusion | flops 6144480256 | bytes 21440000 | tf_op jit(solution)/shard_map/dot_general | solution.py:17
  199.1 0.0 copy-start
  199.1 4.6 %reshape.90 = bf16[480000,1]{0,1:T(2,128)(2,1)} reshape(bf16[400,1200]{1,0:T(8,128)(2,1)S(1)} %convolution_convert_fusion) | data formatting | bytes 1920000 | tf_op jit(solution)/shard_map/reshape;reshape | solution.py:22
  203.7 0.0 copy-done
  203.7 5.6 %convolution_bitcast_fusion = f32[2]{0:T(128)S(1)} fusion(bf16[480000,1]{0,1:T(2,128)(2,1)} %reshape.90, bf16[2,480000]{1,0:T(2,128)(2,1)S(1)} %copy-done), kind=kOutput, calls=%fused_computation.6 | convolution fusion | flops 1920000 | bytes 2880008 | tf_op jit(solution)/shard_map/kn,n->k/dot_general | solution.py:21
  209.3 2.0 reshape.88
  211.3 77.7 %psum.14 = f32[2]{0:T(128)S(1)} all-reduce(f32[2]{0:T(128)S(1)} %convolution_bitcast_fusion), channel_id=1, replica_groups=mesh['slab'=4,'panel'=64] {'slab','panel'}, use_global_device_ids=true, to_apply=%region_0.1 | all-reduce | flops 2 | bytes 16 | tf_op jit(solution)/shard_map/psum | solution.py:41
  289.0 0.0 copy-start.2
  289.0 0.7 fusion.7
  289.6 7.3 %multiply_reduce_fusion = (f32[]{:T(128)}, f32[400,4,300]{2,1,0:T(4,128)S(1)}) fusion(f32[400]{0:T(512)S(1)} %add.70, f32[4,300]{1,0:T(4,128)S(1)} %broadcast_add_fusion, bf16[2,400,4,300]{3,2,1,0:T(4,128)(2,1)} %param.11, f32[]{:T(128)} %bitcast.5, f32[]{:T(128)} %bitcast.3, bf16[400,4,300]{2,1,0:T(4,128)(2,1)} %param.12, f32[]{:T(128)} %bitcast.22, ...), kind=kLoop, calls=%fused_computation.5 | loop fusion | flops 7679999 | bytes 5766416 | tf_op jit(solution)/shard_map/reduce_sum | solution.py:46
  296.9 0.0 copy-done.2
  296.9 72.7 %psum.15 = f32[]{:T(128)} all-reduce(f32[]{:T(128)} %get-tuple-element.5), channel_id=1, replica_groups=mesh['slab'=4,'panel'=64] {'slab','panel'}, use_global_device_ids=true, to_apply=%region_4.5 | all-reduce | flops 1 | bytes 8 | tf_op jit(solution)/shard_map/psum | solution.py:46
  370.3 1.5 multiply_convert_fusion
  (2 shorter events, 0.0 us)
Async XLA Ops:
  5.1 157.7 %all-to-all-start = ((bf16[64,400,100]{2,1,0:T(8,128)(2,1)}), bf16[64,400,100]{2,1,0:T(8,128)(2,1)}, u32[]{:S(2)}, u32[]{:S(2)}) async-start(bf16[64,400,100]{2,1,0:T(8,128)(2,1)} %stack.2), calls=%async_computation | async-start | bytes 13107200 | tf_op jit(solution)/shard_map/all_to_all | solution.py:15
  55.3 4.7 %copy-start.3 = (f32[40]{0:T(128)S(1)}, f32[40]{0:T(128)}, u32[]{:S(2)}) copy-start(f32[40]{0:T(128)} %param.13) | copy-start | bytes 484
  55.3 4.8 %copy-start.1 = (f32[300]{0:T(512)S(1)}, f32[300]{0:T(512)}, u32[]{:S(2)}) copy-start(f32[300]{0:T(512)} %param.14) | copy-start | bytes 3604
  199.1 4.6 %copy-start = (bf16[2,480000]{1,0:T(2,128)(2,1)S(1)}, bf16[2,480000]{1,0:T(2,128)(2,1)}, u32[]{:S(2)}) copy-start(bf16[2,480000]{1,0:T(2,128)(2,1)} %reshape.89) | copy-start | bytes 5760004
  289.0 7.9 %copy-start.2 = (f32[2]{0:T(128)}, f32[2]{0:T(128)S(1)}, u32[]{:S(2)}) copy-start(f32[2]{0:T(128)S(1)} %psum.14) | copy-start | bytes 28
